TPU v7x, 32 devices: a whole 2x2x4 slice. The times are simulated.
32 devices in a mesh: dp: 8 (over y, x, core), fsdp: 4 (over z).
Axes of the slice: x: 2, y: 2, z: 4, core: 2. Of those that a mesh axis runs over, the one named last changes fastest.
Arguments:
- inputs: bfloat16 [32, 8, 12, 6, 6, 256], P(('dp', 'fsdp')), may hold values from -6 to 6
- cotangent: bfloat16 [32, 8, 12, 6, 6, 256], P(('dp', 'fsdp')), may hold values from -6 to 6
- lengths: int32 [32], P(('dp', 'fsdp')), may hold values from 2 to 8
- face_table: int32 [12, 4], replicated, may hold values from 0 to 11
- w_first: float32 [2304, 256], P('fsdp'), may hold values from -0.125 to 0.125
- w_second: float32 [2304, 256], P('fsdp'), may hold values from -0.125 to 0.125
- w_skip: float32 [256, 256], P('fsdp'), may hold values from -0.375 to 0.375
- mom_first: float32 [2304, 256], P('fsdp'), may hold values from -64 to 64
- sq_first: float32 [2304, 256], P('fsdp'), may hold values from 12.16512 to 48.66048
- mom_second: float32 [2304, 256], P('fsdp'), may hold values from -64 to 64
- sq_second: float32 [2304, 256], P('fsdp'), may hold values from 12.16512 to 48.66048
- mom_skip: float32 [256, 256], P('fsdp'), may hold values from -160 to 160
- sq_skip: float32 [256, 256], P('fsdp'), may hold values from 68.56704 to 276.48
Outputs:
- output: bfloat16 [32, 8, 12, 6, 6, 256], P(('dp', 'fsdp'))
- grad_inputs: float32 [32, 8, 12, 6, 6, 256], P(('dp', 'fsdp'))
- new_first: float32 [2304, 256], P('fsdp')
- new_mom_first: float32 [2304, 256], P('fsdp')
- new_sq_first: float32 [2304, 256], P('fsdp')
- new_second: float32 [2304, 256], P('fsdp')
- new_mom_second: float32 [2304, 256], P('fsdp')
- new_sq_second: float32 [2304, 256], P('fsdp')
- new_skip: float32 [256, 256], P('fsdp')
- new_mom_skip: float32 [256, 256], P('fsdp')
- new_sq_skip: float32 [256, 256], P('fsdp')
All inputs are finite; a program needn't handle non-finite values.
Results may differ from a plain program's by a relative error of at most 0.019.
Values may be sent and summed in bfloat16 or wider, within the bound.
No kernel may reach another device: no remote copies, remote signals or barrier semaphores. Data moves between devices by JAX's collectives and lax.ppermute only.
A program may use at most 256 MiB of HBM per device.

v0:
```python
import jax
import jax.numpy as jnp
from jax import lax
from jax.sharding import PartitionSpec as P

C = 256
STEP_COUNT = 10
tap_offsets = [(row_off, col_off) for row_off in range(3) for col_off in range(3)]


def face_hots(face_table, dtype):
    faces = face_table.shape[0]
    labels = jnp.arange(faces, dtype=jnp.int32)
    return [
        (face_table[:, corner_side][:, None] == labels[None, :]).astype(dtype)
        for corner_side in range(4)
    ]


def pad_faces(field, hots):

    def route(matrix, edge, form):
        return jnp.einsum(form, matrix, edge, preferred_element_type=jnp.float32).astype(
            jnp.bfloat16
        )

    north = route(hots[0], field[:, :, -1], "fh,rhwc->rfwc")
    east = route(hots[1], field[:, :, :, 0], "fh,rhwc->rfwc")
    south = route(hots[2], field[:, :, 0], "fh,rhwc->rfwc")
    west = route(hots[3], field[:, :, :, -1], "fh,rhwc->rfwc")
    middle = jnp.concatenate([west[:, :, :, None], field, east[:, :, :, None]], axis=3)
    top_row = jnp.pad(north, ((0, 0), (0, 0), (1, 1), (0, 0)))
    bottom_row = jnp.pad(south, ((0, 0), (0, 0), (1, 1), (0, 0)))
    return jnp.concatenate([top_row[:, :, None], middle, bottom_row[:, :, None]], axis=2)


def unpad_back(spread, hots):
    highest = lax.Precision.HIGHEST
    inner = spread[:, :, 1:-1, 1:-1]
    inner = inner.at[:, :, -1].add(
        jnp.einsum("fh,rfwc->rhwc", hots[0], spread[:, :, 0, 1:-1], precision=highest)
    )
    inner = inner.at[:, :, :, 0].add(
        jnp.einsum("fh,rfwc->rhwc", hots[1], spread[:, :, 1:-1, -1], precision=highest)
    )
    inner = inner.at[:, :, 0].add(
        jnp.einsum("fh,rfwc->rhwc", hots[2], spread[:, :, -1, 1:-1], precision=highest)
    )
    inner = inner.at[:, :, :, -1].add(
        jnp.einsum("fh,rfwc->rhwc", hots[3], spread[:, :, 1:-1, 0], precision=highest)
    )
    return inner


def conv_apply(padded, weight):
    edge_len = padded.shape[2] - 2
    channels = weight.shape[1]
    taps_weight = weight.reshape(9, channels, channels)
    flat_padded = padded.reshape(-1, channels)
    products = jnp.einsum(
        "pc,tcd->ptd", flat_padded, taps_weight, preferred_element_type=jnp.float32
    )
    products = products.reshape(padded.shape[:4] + (9, channels))
    summed = None
    for tap_index, (row_off, col_off) in enumerate(tap_offsets):
        part = products[:, :, row_off : row_off + edge_len, col_off : col_off + edge_len, tap_index]
        summed = part if summed is None else summed + part
    return summed


def conv_back(padded, grad, weight):
    channels = weight.shape[1]
    taps_weight = weight.reshape(9, channels, channels)
    flat_grad = grad.reshape(-1, channels)
    pulled = jnp.einsum("pd,tcd->ptc", flat_grad, taps_weight, preferred_element_type=jnp.float32)
    pulled = pulled.reshape(grad.shape[:4] + (9, channels))
    spread = None
    placed = []
    for tap_index, (row_off, col_off) in enumerate(tap_offsets):
        widths = ((0, 0), (0, 0), (row_off, 2 - row_off), (col_off, 2 - col_off), (0, 0))
        moved = jnp.pad(pulled[:, :, :, :, tap_index], widths)
        spread = moved if spread is None else spread + moved
        placed.append(jnp.pad(grad, widths))
    stacked = jnp.stack(placed, axis=4).reshape(-1, 9, channels)
    flat_padded = padded.reshape(-1, channels)
    weight_grad = jnp.einsum(
        "pc,ptd->tcd", flat_padded, stacked, preferred_element_type=jnp.float32
    )
    return (weight_grad.reshape(9 * channels, channels), spread)


def gelu_tanh(v):
    return jax.nn.gelu(v, approximate=True)


def forward_pass(fields, hots_low, gathered):
    pad_in = pad_faces(fields, hots_low)
    pre_one = conv_apply(pad_in, gathered[0])
    hidden = gelu_tanh(pre_one).astype(jnp.bfloat16)
    pad_hidden = pad_faces(hidden, hots_low)
    pre_two = conv_apply(pad_hidden, gathered[1])
    return (pad_in, pre_one, pad_hidden, pre_two)


def adamw(weight, moment, square, grad, rate):
    moment_new = 0.9 * moment + 0.1 * grad
    square_new = 0.999 * square + 0.001 * grad * grad
    fix_one = 1.0 - 0.9**STEP_COUNT
    fix_two = 1.0 - 0.999**STEP_COUNT
    weight_new = weight - rate * (
        moment_new / fix_one / (jnp.sqrt(square_new / fix_two) + 1e-08) + 0.01 * weight
    )
    return (weight_new, moment_new, square_new)


def per_device(
    inputs,
    cotangent,
    lengths,
    face_table,
    w_first,
    w_second,
    w_skip,
    mom_first,
    sq_first,
    mom_second,
    sq_second,
    mom_skip,
    sq_skip,
):
    fields = inputs[0]
    channels = fields.shape[-1]
    hots_low = face_hots(face_table, jnp.bfloat16)
    hots_full = face_hots(face_table, jnp.float32)
    low_weights = (
        w_first.astype(jnp.bfloat16),
        w_second.astype(jnp.bfloat16),
        w_skip.astype(jnp.bfloat16),
    )
    gathered = (
        lax.all_gather(low_weights[0], "fsdp", axis=0, tiled=True),
        lax.all_gather(low_weights[1], "fsdp", axis=0, tiled=True),
        lax.all_gather(low_weights[2], "fsdp", axis=0, tiled=True),
    )
    saved = forward_pass(fields, hots_low, gathered)
    flat_fields = fields.reshape(-1, channels)
    skipped = jnp.dot(flat_fields, gathered[2], preferred_element_type=jnp.float32).reshape(
        fields.shape
    )
    output = (gelu_tanh(saved[3]) + skipped).astype(jnp.bfloat16)
    gathered = (
        lax.all_gather(low_weights[0], "fsdp", axis=0, tiled=True),
        lax.all_gather(low_weights[1], "fsdp", axis=0, tiled=True),
        lax.all_gather(low_weights[2], "fsdp", axis=0, tiled=True),
    )
    saved = forward_pass(fields, hots_low, gathered)
    pad_in, pre_one, pad_hidden, pre_two = saved
    live = (jnp.arange(fields.shape[0]) < lengths[0]).astype(jnp.bfloat16)
    grad_out = cotangent[0] * live[:, None, None, None, None]
    flat_out = grad_out.reshape(-1, channels)
    dw_skip = lax.dot_general(
        flat_fields, flat_out, (((0,), (0,)), ((), ())), preferred_element_type=jnp.float32
    )
    gelu_pull_two = jax.vjp(gelu_tanh, pre_two)[1]
    grad_two = gelu_pull_two(grad_out.astype(jnp.float32))[0].astype(jnp.bfloat16)
    dw_second, spread_hidden = conv_back(pad_hidden, grad_two, gathered[1])
    grad_hidden = unpad_back(spread_hidden, hots_full)
    gelu_pull_one = jax.vjp(gelu_tanh, pre_one)[1]
    grad_one = gelu_pull_one(grad_hidden)[0].astype(jnp.bfloat16)
    dw_first, spread_in = conv_back(pad_in, grad_one, gathered[0])
    skip_back = lax.dot_general(
        flat_out, gathered[2], (((1,), (1,)), ((), ())), preferred_element_type=jnp.float32
    )
    grad_inputs = unpad_back(spread_in, hots_full) + skip_back.reshape(fields.shape)
    shards = (
        lax.psum_scatter(
            dw_first.astype(jnp.bfloat16), "fsdp", scatter_dimension=0, tiled=True
        ).astype(jnp.float32),
        lax.psum_scatter(
            dw_second.astype(jnp.bfloat16), "fsdp", scatter_dimension=0, tiled=True
        ).astype(jnp.float32),
        lax.psum_scatter(
            dw_skip.astype(jnp.bfloat16), "fsdp", scatter_dimension=0, tiled=True
        ).astype(jnp.float32),
    )
    rate_conv = (9 * C) ** (-0.5)
    rate_skip = C ** (-0.5)
    totals = (
        lax.psum(shards[0].astype(jnp.bfloat16), "dp").astype(jnp.float32),
        lax.psum(shards[1].astype(jnp.bfloat16), "dp").astype(jnp.float32),
        lax.psum(shards[2].astype(jnp.bfloat16), "dp").astype(jnp.float32),
    )
    first_set = adamw(w_first, mom_first, sq_first, totals[0], rate_conv)
    second_set = adamw(w_second, mom_second, sq_second, totals[1], rate_conv)
    skip_set = adamw(w_skip, mom_skip, sq_skip, totals[2], rate_skip)
    return (
        output[None],
        grad_inputs[None],
        first_set[0],
        first_set[1],
        first_set[2],
        second_set[0],
        second_set[1],
        second_set[2],
        skip_set[0],
        skip_set[1],
        skip_set[2],
    )


def solution(mesh):
    placed = (
        P(("dp", "fsdp"), None, None, None, None, None),
        P(("dp", "fsdp"), None, None, None, None, None),
        P(("dp", "fsdp")),
        P(),
        P("fsdp", None),
        P("fsdp", None),
        P("fsdp", None),
        P("fsdp", None),
        P("fsdp", None),
        P("fsdp", None),
        P("fsdp", None),
        P("fsdp", None),
        P("fsdp", None),
    )
    return jax.shard_map(
        per_device,
        mesh=mesh,
        in_specs=placed,
        out_specs=(
            P(("dp", "fsdp"), None, None, None, None, None),
            P(("dp", "fsdp"), None, None, None, None, None),
            P("fsdp", None),
            P("fsdp", None),
            P("fsdp", None),
            P("fsdp", None),
            P("fsdp", None),
            P("fsdp", None),
            P("fsdp", None),
            P("fsdp", None),
            P("fsdp", None),
        ),
        check_vma=False,
    )
```

profile of v0, /device:TPU:0, one launch (start us, length us, event | category | flops | bytes accessed | tf_op | source)
XLA Modules:
  0.0 511.8 jit_solution(13693216425621798046)
XLA Ops:
  7.9 5.0 fusion.84
  24.7 11.0 %reduce-scatter.10.cloned.1.call-done = bf16[64,256]{1,0:T(8,128)(2,1)} async-done(((bf16[256,256]{1,0:T(8,128)(2,1)}), bf16[64,256]{1,0:T(8,128)(2,1)}) %reduce-scatter.10.cloned.1.call-update) | async-done | bytes 32784 | tf_op jit(solution)/shard_map/reduce_scatter | solution.py:182
  35.7 23.7 %psum.23 = bf16[64,256]{1,0:T(8,128)(2,1)S(1)} all-reduce(bf16[64,256]{1,0:T(8,128)(2,1)} %reduce-scatter.10.cloned.1.call-done), channel_id=1, replica_groups=mesh['dp'=8,'fsdp'=4] {'dp'}, use_global_device_ids=true, to_apply=%region_5.6 | all-reduce | flops 16384 | bytes 65536 | tf_op jit(solution)/shard_map/psum | solution.py:191
  60.2 14.7 %all_gather.14 = bf16[256,256]{1,0:T(8,128)(2,1)} all-gather(bf16[64,256]{1,0:T(8,128)(2,1)S(1)} %get-tuple-element.194), channel_id=1, replica_groups=mesh['dp'=8,'fsdp'=4] {'fsdp'}, dimensions={0}, use_global_device_ids=true | all-gather | bytes 163840 | tf_op jit(solution)/shard_map/all_gather | solution.py:143
  74.8 24.0 %fusion.33 = f32[8,12,8,8,9,256]{5,3,4,2,1,0:T(8,128)} fusion(bf16[9,256,256,1,1,1]{2,1,0,5,4,3:T(8,128)(2,1)} %bitcast.404, bf16[8,12,8,8,256,1]{4,1,3,0,2,5:T(8,128)(2,1)} %maximum_bitcast_fusion), kind=kOutput, calls=%fused_computation.102 | convolution fusion | flops 7247757312 | bytes 60948480 | tf_op jit(solution)/shard_map/pc,tcd->ptd/dot_general | solution.py:60
  98.8 17.8 %multiply_convert_fusion = (bf16[8,12,6,6,256]{4,3,2,1,0:T(8,128)(2,1)S(1)}, f32[8,12,6,6,256]{4,3,2,1,0:T(8,128)}) fusion(f32[8,12,8,8,9,256]{5,3,4,2,1,0:T(8,128)} %fusion.33), kind=kLoop, calls=%fused_computation.78 | loop fusion | flops 15040512 | bytes 37158912 | tf_op jit(solution)/shard_map/convert_element_type | solution.py:99
  123.0 22.2 %fusion.115 = f32[8,12,8,8,9,256]{5,3,2,1,0,4:T(8,128)} fusion(bf16[9,256,256,1,1,1]{2,1,5,4,3,0:T(8,128)(2,1)} %bitcast.402, bf16[8,12,1,8,256]{4,3,2,1,0:T(8,128)(2,1)} %copy.301, bf16[8,12,6,1,256]{4,3,2,1,0:T(2,128)(2,1)S(1)} %copy.296, bf16[8,12,6,6,256]{4,3,2,1,0:T(8,128)(2,1)S(1)} %get-tuple-element.164, bf16[8,12,6,1,256]{4,3,2,1,0:T(2,128)(2,1)S(1)} %copy.295, ...), kind=kOutput, calls=%fused_computation.210 | convolution fusion | flops 7263485952 | bytes 60948480 | tf_op jit(solution)/shard_map/pc,tcd->ptd/dot_general | solution.py:60
  145.3 18.2 %fusion.7 = (bf16[8,12,6,6,256]{4,3,2,1,0:T(8,128)(2,1)S(1)}, f32[8,12,6,6,1,256]{5,3,2,1,0,4:T(8,128)}) fusion(bf16[8]{0:T(256)(128)(2,1)S(1)} %copy-done.29, bf16[1,8,12,6,6,256]{5,1,4,3,2,0:T(8,128)(2,1)S(1)} %copy-done.1, f32[8,12,8,8,9,256]{5,3,2,1,0,4:T(8,128)} %fusion.115), kind=kLoop, calls=%fused_computation.19 | loop fusion | flops 26542080 | bytes 38928400 | tf_op jit(solution)/shard_map/convert_element_type | solution.py:165
  163.5 19.7 %fusion.40 = f32[8,12,6,6,9,256]{5,3,2,1,0,4:T(8,128)} fusion(bf16[9,256,256,1,1,1]{2,1,5,4,3,0:T(8,128)(2,1)S(1)} %bitcast.403, f32[8,12,6,6,1,256]{5,3,2,1,0,4:T(8,128)} %get-tuple-element.163, bf16[1,8,12,6,6,256]{5,1,4,3,2,0:T(8,128)(2,1)} %param.30, bf16[8]{0:T(256)(128)(2,1)} %copy-done.28), kind=kOutput, calls=%fused_computation.113 | convolution fusion | flops 4098097152 | bytes 38338576 | tf_op jit(solution)/shard_map/pd,tcd->ptc/dot_general | solution.py:75
  183.2 30.6 %slice_bitcast_fusion.17 = (f32[8,12,6,6,256]{4,3,2,1,0:T(8,128)}, f32[8,12,6,6,256]{4,3,2,1,0:T(8,128)}, f32[8,12,6,6,256]{4,3,2,1,0:T(8,128)}, f32[8,12,6,6,25...) fusion(f32[8,12,6,6,9,256]{5,3,2,1,0,4:T(8,128)} %fusion.40), kind=kLoop, calls=%fused_computation.56 | loop fusion | bytes 63700992 | tf_op jit(solution)/shard_map/squeeze | solution.py:81
  213.8 18.5 %pad_add_fusion.1 = f32[8,12,8,8,256]{4,3,2,1,0:T(8,128)} fusion(f32[8,12,6,6,256]{4,3,2,1,0:T(8,128)} %get-tuple-element.183, f32[8,12,6,6,256]{4,3,2,1,0:T(8,128)} %get-tuple-element.176, f32[8,12,6,6,256]{4,3,2,1,0:T(8,128)} %get-tuple-element.177, f32[8,12,6,6,256]{4,3,2,1,0:T(8,128)} %get-tuple-element.178, f32[8,12,6,6,256]{4,3,2,1,0:T(8,128)} %get-tuple-element.179, ...), kind=kLoop, calls=%fused_computation.7 | loop fusion | flops 12582912 | bytes 38141952 | tf_op jit(solution)/shard_map/add | solution.py:82
  232.3 4.9 fusion.175
  237.2 2.7 slice_bitcast_fusion.26
  239.9 5.3 %slice.563 = f32[8,12,6,6,256]{4,3,2,1,0:T(8,128)} slice(f32[8,12,8,8,256]{4,3,2,1,0:T(8,128)} %pad_add_fusion.1), slice={[0:8], [0:12], [1:7], [1:7], [0:256]} | slice | bytes 7077888 | tf_op jit(solution)/shard_map/slice | solution.py:39
  267.0 13.9 %bitcast_convert_fusion = bf16[9,256,256]{1,2,0:T(8,128)(2,1)} fusion(bf16[8,12,8,8,9,256]{5,3,2,1,0,4:T(8,128)(2,1)} %bitcast_dynamic-update-slice_fusion, bf16[8,12,1,8,256]{4,3,2,1,0:T(8,128)(2,1)S(1)} %copy-done.19, bf16[8,12,6,1,256]{4,3,2,1,0:T(2,128)(2,1)S(1)} %copy-done.16, bf16[8,12,6,6,256]{4,3,2,1,0:T(8,128)(2,1)S(1)} %copy-done.3, ...), kind=kOutput, calls=%fused_computation.111 | convolution fusion | flops 7264075776 | bytes 32636928 | tf_op jit(solution)/shard_map/pc,ptd->tcd/dot_general | solution.py:86
  283.8 2.6 fusion.90
  286.4 3.2 slice_add_fusion.19
  289.6 13.0 %scatter-add.29 = f32[8,12,6,6,256]{4,3,2,1,0:T(8,128)} dynamic-update-slice(f32[8,12,6,6,256]{4,3,2,1,0:T(8,128)} %fusion.90, f32[8,12,6,1,256]{4,3,2,1,0:T(1,128)S(1)} %slice_add_fusion.19, s32[]{:T(128)} %constant.226.clone.1, s32[]{:T(128)} %constant.226.clone.1, s32[]{:T(128)} %constant.226.clone.1, s32[]{:T(128)} %constant.226.clone.1, s32[]{:T(128)} %constant.226.clone.1) | dynamic-update-slice | bytes 1179652 | tf_op jit(solution)/shard_map/scatter-add | solution.py:43
  305.1 3.4 slice_add_fusion.18
  308.5 13.0 %scatter-add.31 = f32[8,12,6,6,256]{4,3,2,1,0:T(8,128)} dynamic-update-slice(f32[8,12,6,6,256]{4,3,2,1,0:T(8,128)} %fusion.89, f32[8,12,6,1,256]{4,3,2,1,0:T(1,128)S(1)} %slice_add_fusion.18, s32[]{:T(128)} %constant.226.clone.1, s32[]{:T(128)} %constant.226.clone.1, s32[]{:T(128)} %constant.226.clone.1, s32[]{:T(128)} %constant.227.clone.1, s32[]{:T(128)} %constant.226.clone.1) | dynamic-update-slice | bytes 1179652 | tf_op jit(solution)/shard_map/scatter-add | solution.py:49
  321.5 5.5 %fusion.16 = bf16[8,12,6,6,256]{4,3,2,1,0:T(8,128)(2,1)S(1)} fusion(f32[8,12,6,6,256]{4,3,2,1,0:T(8,128)} %get-tuple-element.165, f32[8,12,6,6,256]{4,3,2,1,0:T(8,128)} %scatter-add.31), kind=kLoop, calls=%fused_computation.28 | loop fusion | flops 17694720 | bytes 8847360 | tf_op jit(solution)/shard_map/convert_element_type | solution.py:169
  348.7 16.7 %fusion.43 = f32[8,12,6,6,9,256]{5,1,4,3,2,0:T(8,128)} fusion(bf16[9,256,256,1,1,1]{2,1,0,5,4,3:T(8,128)(2,1)S(1)} %bitcast.405, bf16[8,12,6,6,256,1]{4,3,2,1,0,5:T(8,128)(2,1)S(1)} %bitcast.397), kind=kOutput, calls=%fused_computation.116 | convolution fusion | flops 4076863488 | bytes 34799616 | tf_op jit(solution)/shard_map/pd,tcd->ptc/dot_general | solution.py:75
  365.3 31.7 %slice_bitcast_fusion.8 = (f32[8,12,6,6,256]{4,1,3,2,0:T(8,128)}, f32[8,12,6,6,256]{4,1,3,2,0:T(8,128)}, f32[8,12,6,6,256]{4,1,3,2,0:T(8,128)}, f32[8,12,6,6,256...) fusion(f32[8,12,6,6,9,256]{5,1,4,3,2,0:T(8,128)} %fusion.43), kind=kLoop, calls=%fused_computation.47 | loop fusion | bytes 63700992 | tf_op jit(solution)/shard_map/squeeze | solution.py:81
  397.0 15.3 %bitcast_convert_fusion.1 = bf16[9,256,256]{1,2,0:T(8,128)(2,1)} fusion(bf16[8,12,8,8,9,256]{5,3,2,1,0,4:T(8,128)(2,1)} %bitcast_dynamic-update-slice_fusion.9, bf16[8,12,8,8,256,1]{4,1,3,0,2,5:T(8,128)(2,1)} %maximum_bitcast_fusion), kind=kOutput, calls=%fused_computation.112 | convolution fusion | flops 7248347136 | bytes 32636928 | tf_op jit(solution)/shard_map/pc,ptd->tcd/dot_general | solution.py:86
  412.4 4.9 fusion.53
  417.3 3.1 copy.352
  420.4 14.8 %pad_add_fusion = f32[8,12,8,8,256]{4,1,3,2,0:T(8,128)S(1)} fusion(f32[8,12,6,6,256]{4,1,3,2,0:T(8,128)} %get-tuple-element.173, f32[8,12,6,6,256]{4,1,3,2,0:T(8,128)} %get-tuple-element.174, f32[8,12,6,6,256]{4,1,3,2,0:T(8,128)} %get-tuple-element.167, f32[8,12,6,6,256]{4,1,3,2,0:T(8,128)} %get-tuple-element.168, f32[8,12,6,6,256]{4,1,3,2,0:T(8,128)} %get-tuple-element.169, ...), kind=kLoop, calls=%fused_computation | loop fusion | flops 12582912 | bytes 38141952 | tf_op jit(solution)/shard_map/add | solution.py:82
  435.3 2.7 slice.581
  439.4 2.6 fusion.63
  447.1 3.3 add_bitcast_fusion
  450.4 3.8 copy.353
  454.3 45.6 %all-reduce.43.cloned.1.call-done = (bf16[576,256]{1,0:T(8,128)(2,1)}, bf16[576,256]{1,0:T(8,128)(2,1)}) async-done(((bf16[576,256]{1,0:T(8,128)(2,1)}, bf16[576,256]{1,0:T(8,128)(2,1)}), (bf16[576,256]{1,0:T(8,128)(2,1)}, bf16[576,256]{1,0:T(8,128)(2,1)})) %all-reduce.43.cloned.1.call-update) | async-done | bytes 589840 | tf_op jit(solution)/shard_map/psum | solution.py:189
  (139 shorter events, 78.9 us)
Async XLA Ops:
  7.2 28.6 %reduce-scatter.10.cloned.1.call-start = ((), (), s32[]{:S(2)}) async-start(), calls=%async_computation.7 | async-start | bytes 163840 | tf_op jit(solution)/shard_map/reduce_scatter | solution.py:182
  7.9 10.1 %copy-start.28 = (bf16[8]{0:T(256)(128)(2,1)}, bf16[8]{0:T(256)(128)(2,1)S(1)}, u32[]{:S(2)}) copy-start(bf16[8]{0:T(256)(128)(2,1)S(1)} %compare_convert_fusion) | copy-start | bytes 52
  7.9 5.9 %copy-start.9 = (f32[576,256]{1,0:T(8,128)S(1)}, f32[576,256]{1,0:T(8,128)}, u32[]{:S(2)}) copy-start(f32[576,256]{1,0:T(8,128)} %param.33) | copy-start | bytes 1769476
  7.9 6.7 %copy-start.11 = (f32[576,256]{1,0:T(8,128)S(1)}, f32[576,256]{1,0:T(8,128)}, u32[]{:S(2)}) copy-start(f32[576,256]{1,0:T(8,128)} %param.34) | copy-start | bytes 1769476
  12.9 5.1 copy-start
  13.7 61.1 %all-gather.3.cloned.1.call-start = ((), (), s32[]{:S(2)}) async-start(), calls=%async_computation.3 | async-start | bytes 1474560 | tf_op jit(solution)/shard_map/all_gather | solution.py:141
  14.5 5.6 %copy-start.30 = (s32[12,4]{0,1:T(4,128)S(1)}, s32[12,4]{0,1:T(4,128)}, u32[]{:S(2)}) copy-start(s32[12,4]{0,1:T(4,128)} %param.32) | copy-start | bytes 580
  14.5 107.7 %all-gather.5.cloned.1.call-start = ((), (), s32[]{:S(2)}) async-start(), calls=%async_computation.4 | async-start | bytes 1474560 | tf_op jit(solution)/shard_map/all_gather | solution.py:142
  15.4 431.7 %reduce-scatter.8.cloned.1.call-start = ((), (), s32[]{:S(2)}) async-start(), calls=%async_computation.6 | async-start | bytes 1474560 | tf_op jit(solution)/shard_map/reduce_scatter | solution.py:179
  22.1 37.4 %copy-start.25 = (f32[64,256]{1,0:T(8,128)S(1)}, f32[64,256]{1,0:T(8,128)}, u32[]{:S(2)}) copy-start(f32[64,256]{1,0:T(8,128)} %param.35) | copy-start | bytes 196612
  22.1 37.4 %copy-start.26 = (f32[64,256]{1,0:T(8,128)S(1)}, f32[64,256]{1,0:T(8,128)}, u32[]{:S(2)}) copy-start(f32[64,256]{1,0:T(8,128)} %param.40) | copy-start | bytes 196612
  22.1 37.4 %copy-start.27 = (f32[64,256]{1,0:T(8,128)S(1)}, f32[64,256]{1,0:T(8,128)}, u32[]{:S(2)}) copy-start(f32[64,256]{1,0:T(8,128)} %param.41) | copy-start | bytes 196612
  116.6 5.7 %copy-start.2 = (bf16[8,12,6,6,256]{4,3,2,1,0:T(8,128)(2,1)}, bf16[8,12,6,6,256]{4,3,2,1,0:T(8,128)(2,1)S(1)}, u32[]{:S(2)}) copy-start(bf16[8,12,6,6,256]{4,3,2,1,0:T(8,128)(2,1)S(1)} %get-tuple-element.164) | copy-start | bytes 5308420
  123.0 22.3 %copy-start.1 = (bf16[1,8,12,6,6,256]{5,1,4,3,2,0:T(8,128)(2,1)S(1)}, bf16[1,8,12,6,6,256]{5,1,4,3,2,0:T(8,128)(2,1)}, u32[]{:S(2)}) copy-start(bf16[1,8,12,6,6,256]{5,1,4,3,2,0:T(8,128)(2,1)} %param.30) | copy-start | bytes 5308420
  123.0 22.3 %copy-start.29 = (bf16[8]{0:T(256)(128)(2,1)S(1)}, bf16[8]{0:T(256)(128)(2,1)}, u32[]{:S(2)}) copy-start(bf16[8]{0:T(256)(128)(2,1)} %copy-done.28) | copy-start | bytes 52
  145.3 18.2 %copy-start.5 = (bf16[2304,256]{1,0:T(8,128)(2,1)S(1)}, bf16[2304,256]{1,0:T(8,128)(2,1)}, u32[]{:S(2)}) copy-start(bf16[2304,256]{1,0:T(8,128)(2,1)} %all-gather.5.cloned.1.call-done) | copy-start | bytes 3538948
  262.0 4.9 copy-start.3
  262.0 4.9 copy-start.14
  262.0 4.9 copy-start.16
  262.0 4.9 copy-start.18
  262.0 4.9 copy-start.19
  280.9 166.2 %reduce-scatter.6.cloned.1.call-start = ((), (), s32[]{:S(2)}) async-start(), calls=%async_computation.5 | async-start | bytes 1474560 | tf_op jit(solution)/shard_map/reduce_scatter | solution.py:176
  397.0 15.4 %copy-start.17 = (bf16[1,8,12,6,6,256]{5,1,4,3,2,0:T(8,128)(2,1)S(1)}, bf16[1,8,12,6,6,256]{5,1,4,3,2,0:T(8,128)(2,1)}, u32[]{:S(2)}) copy-start(bf16[1,8,12,6,6,256]{5,1,4,3,2,0:T(8,128)(2,1)} %param.29) | copy-start | bytes 5308420
  397.0 15.4 %copy-start.24 = (bf16[256,256]{1,0:T(8,128)(2,1)S(1)}, bf16[256,256]{1,0:T(8,128)(2,1)}, u32[]{:S(2)}) copy-start(bf16[256,256]{1,0:T(8,128)(2,1)} %all_gather.14) | copy-start | bytes 393220
  412.4 87.5 %all-reduce.43.cloned.1.call-start = ((), (), s32[]{:S(2)}) async-start(), calls=%async_computation.8 | async-start | bytes 1179648 | tf_op jit(solution)/shard_map/psum | solution.py:189
  438.0 9.1 %copy-start.4 = (bf16[8,12,6,6,256]{4,3,2,1,0:T(8,128)(2,1)S(1)}, bf16[8,12,6,6,256]{4,3,2,1,0:T(8,128)(2,1)}, u32[]{:S(2)}) copy-start(bf16[8,12,6,6,256]{4,3,2,1,0:T(8,128)(2,1)} %fusion.39) | copy-start | bytes 5308420
  450.4 49.5 %copy-start.10 = (f32[576,256]{1,0:T(8,128)S(1)}, f32[576,256]{1,0:T(8,128)}, u32[]{:S(2)}) copy-start(f32[576,256]{1,0:T(8,128)} %param.33) | copy-start | bytes 1769476
  450.4 49.5 %copy-start.20 = (f32[576,256]{1,0:T(8,128)S(1)}, f32[576,256]{1,0:T(8,128)}, u32[]{:S(2)}) copy-start(f32[576,256]{1,0:T(8,128)} %param.36) | copy-start | bytes 1769476
  450.4 49.5 %copy-start.21 = (f32[576,256]{1,0:T(8,128)S(1)}, f32[576,256]{1,0:T(8,128)}, u32[]{:S(2)}) copy-start(f32[576,256]{1,0:T(8,128)} %param.37) | copy-start | bytes 1769476
  450.4 51.9 %copy-start.12 = (f32[576,256]{1,0:T(8,128)S(1)}, f32[576,256]{1,0:T(8,128)}, u32[]{:S(2)}) copy-start(f32[576,256]{1,0:T(8,128)} %param.34) | copy-start | bytes 1769476
  450.4 51.9 %copy-start.22 = (f32[576,256]{1,0:T(8,128)S(1)}, f32[576,256]{1,0:T(8,128)}, u32[]{:S(2)}) copy-start(f32[576,256]{1,0:T(8,128)} %param.38) | copy-start | bytes 1769476
  450.4 51.9 %copy-start.23 = (f32[576,256]{1,0:T(8,128)S(1)}, f32[576,256]{1,0:T(8,128)}, u32[]{:S(2)}) copy-start(f32[576,256]{1,0:T(8,128)} %param.39) | copy-start | bytes 1769476
  (5 other events, 10.3 us)
Sparse Core Ops, SparseCore 0:
  13.8 21.8 reduce-scatter.9
  38.0 30.0 all-gather.2
  70.2 29.5 all-gather.4
  281.0 26.5 reduce-scatter.7
  412.5 26.7 reduce-scatter.5
  447.2 52.5 all-reduce.42
where the time goes:
time: 519 us; the launch traced here: 512 us
  local copies, waits for them, and re-layouts  163 us (31%)
  matrix products  139 us (27%)
  other arithmetic  98.3 us (19%)
  waiting for transfers between devices  56.7 us (11%)
  blocking collectives  38.4 us (7%)
  between operations  15.6 us (3%)
    squeeze x2, local copies, waits for them, and re-layouts, conv_back(): moved = jnp.pad(pulled[:, :, :, :, tap_index], widths)  62.2 us
    unnamed x82, local copies, waits for them, and re-layouts  49.7 us
    dot_general x2, matrix products, conv_apply(): jnp.einsum('pc,tcd->ptd', flat_padded, taps_weight, preferred_element_typ...  46.2 us
    psum x1, waiting for transfers between devices, per_device(): lax.psum(shards[0].astype(jnp.bfloat16), 'dp').astype(jnp.float32)  45.6 us
    dot_general x2, matrix products, conv_back(): jnp.einsum('pd,tcd->ptc', flat_grad, taps_weight, preferred_element_type=...  36.3 us
    add x2, other arithmetic, conv_back(): spread = moved if spread is None else spread + moved  33.3 us
    dot_general x2, matrix products, conv_back(): jnp.einsum('pc,ptd->tcd', flat_padded, stacked, preferred_element_type=jn...  29.2 us
    psum x1, blocking collectives, per_device(): lax.psum(shards[2].astype(jnp.bfloat16), 'dp').astype(jnp.float32)  23.7 us
  transfers between devices with their start and end apart: 6, of which 2 were waited for; matrix products, arithmetic and copies ran while one was open for 45% of the time, Pallas kernels for 0%

commit v1 on v0

--- a/solution.py
+++ b/solution.py
@@ -6,6 +6,28 @@
 C = 256
 STEP_COUNT = 10
 tap_offsets = [(row_off, col_off) for row_off in range(3) for col_off in range(3)]
+
+
+def meet_rows(obj, group_axis, axis_k):
+    piece_next = jax.lax.psum(1, axis_name=group_axis)
+    tall, n_now, r1 = (piece_next, jax.lax.axis_index(group_axis), obj.shape[axis_k])
+    samples = [(pp, (pp + 1) % tall) for pp in range(tall)]
+    local_now = jnp.zeros((*obj.shape[:axis_k], tall * r1, *obj.shape[axis_k + 1 :]), obj.dtype)
+    found = [(pp, (pp - 1) % tall) for pp in range(tall)]
+    lower = next_value = obj
+    local_now = lax.dynamic_update_slice_in_dim(local_now, obj, n_now * r1, axis=axis_k)
+    known = tall // 2
+    for dev_j in tuple(range(1, known + 1)):
+        lower = jax.lax.ppermute(lower, axis_name=group_axis, perm=samples)
+        local_now = lax.dynamic_update_slice_in_dim(
+            local_now, lower, (n_now - dev_j) % tall * r1, axis=axis_k
+        )
+        if dev_j < tall - known:
+            next_value = jax.lax.ppermute(next_value, axis_name=group_axis, perm=found)
+            local_now = lax.dynamic_update_slice_in_dim(
+                local_now, next_value, (n_now + dev_j) % tall * r1, axis=axis_k
+            )
+    return local_now
 
 
 def face_hots(face_table, dtype):
@@ -140,7 +162,7 @@
     gathered = (
         lax.all_gather(low_weights[0], "fsdp", axis=0, tiled=True),
         lax.all_gather(low_weights[1], "fsdp", axis=0, tiled=True),
-        lax.all_gather(low_weights[2], "fsdp", axis=0, tiled=True),
+        meet_rows(low_weights[2], "fsdp", 0),
     )
     saved = forward_pass(fields, hots_low, gathered)
     flat_fields = fields.reshape(-1, channels)

time: 519 us -> 544 us (1.048)
  local copies, waits for them, and re-layouts: 163 us -> 182 us
  other arithmetic: 98.3 us -> 105 us
    reduce_scatter x1, waiting for transfers between devices: 11 us -> 0.01 us  [per_device(): lax.psum_scatter(dw_skip.astype(jnp.bfloat16), 'fsdp', scatter_dimension=...]
    ppermute x0 -> x3, starting transfers between devices: none -> 5.82 us  [the longest x1 5.05 us: meet_rows(): next_value = jax.lax.ppermute(next_value, axis_name=group_axis, perm=found)]
    unnamed x82 -> x91, local copies, waits for them, and re-layouts: 49.7 us -> 52 us
  transfers between devices with their start and end apart: 6 -> 9, of which waited for: 2 -> 2; matrix products, arithmetic and copies ran while one was open for 45% -> 47% of each run, Pallas kernels for 0% -> 0%
where the time goes in v1:
time: 544 us; the launch traced here: 535 us
  local copies, waits for them, and re-layouts  182 us (33%)
  matrix products  135 us (25%)
  other arithmetic  105 us (19%)
  waiting for transfers between devices  51.4 us (9%)
  blocking collectives  40.5 us (7%)
  between operations  15.6 us (3%)
  starting transfers between devices  6.07 us (1%)
    squeeze x2, local copies, waits for them, and re-layouts, conv_back(): moved = jnp.pad(pulled[:, :, :, :, tap_index], widths)  62.2 us
    unnamed x91, local copies, waits for them, and re-layouts  52 us
    psum x1, waiting for transfers between devices, per_device(): lax.psum(shards[0].astype(jnp.bfloat16), 'dp').astype(jnp.float32)  47 us
    dot_general x2, matrix products, conv_apply(): jnp.einsum('pc,tcd->ptd', flat_padded, taps_weight, preferred_element_typ...  45.8 us
    dot_general x2, matrix products, conv_back(): jnp.einsum('pd,tcd->ptc', flat_grad, taps_weight, preferred_element_type=...  36.3 us
    add x2, other arithmetic, conv_back(): spread = moved if spread is None else spread + moved  33.5 us
    dot_general x2, matrix products, conv_back(): jnp.einsum('pc,ptd->tcd', flat_padded, stacked, preferred_element_type=jn...  29.2 us
    psum x1, blocking collectives, per_device(): lax.psum(shards[2].astype(jnp.bfloat16), 'dp').astype(jnp.float32)  23.9 us
  transfers between devices with their start and end apart: 9, of which 2 were waited for; matrix products, arithmetic and copies ran while one was open for 47% of the time, Pallas kernels for 0%

profile of v1, /device:TPU:0, one launch (start us, length us, event | category | flops | bytes accessed | tf_op | source)
XLA Modules:
  0.0 535.4 jit_solution(11358094174102996031)
XLA Ops:
  7.9 5.0 fusion.79
  16.0 5.0 collective-permute-start.1
  29.4 4.1 reshape_squeeze.3
  41.0 16.6 %all_gather.13 = bf16[256,256]{1,0:T(8,128)(2,1)} all-gather(bf16[64,256]{1,0:T(8,128)(2,1)} %get-tuple-element.167), channel_id=1, replica_groups=mesh['dp'=8,'fsdp'=4] {'fsdp'}, dimensions={0}, use_global_device_ids=true | all-gather | bytes 163840 | tf_op jit(solution)/shard_map/all_gather | solution.py:176
  59.9 4.3 collective-permute-done.2
  64.9 2.9 copy.311
  67.8 4.9 reshape.701
  72.7 23.9 %psum.23 = bf16[64,256]{1,0:T(8,128)(2,1)S(1)} all-reduce(bf16[64,256]{1,0:T(8,128)(2,1)} %reduce-scatter.10.cloned.1.call-done), channel_id=1, replica_groups=mesh['dp'=8,'fsdp'=4] {'dp'}, use_global_device_ids=true, to_apply=%region_5.6 | all-reduce | flops 16384 | bytes 65536 | tf_op jit(solution)/shard_map/psum | solution.py:213
  97.3 23.2 %fusion.33 = f32[8,12,8,8,9,256]{5,3,4,2,1,0:T(8,128)} fusion(bf16[9,256,256,1,1,1]{2,1,0,5,4,3:T(8,128)(2,1)} %bitcast.402, bf16[8,12,8,8,256,1]{4,1,3,0,2,5:T(8,128)(2,1)} %maximum_bitcast_fusion), kind=kOutput, calls=%fused_computation.103 | convolution fusion | flops 7247757312 | bytes 60948480 | tf_op jit(solution)/shard_map/pc,tcd->ptd/dot_general | solution.py:82
  120.5 17.8 %multiply_convert_fusion = (bf16[8,12,6,6,256]{4,3,2,1,0:T(8,128)(2,1)S(1)}, f32[8,12,6,6,256]{4,3,2,1,0:T(8,128)}) fusion(f32[8,12,8,8,9,256]{5,3,4,2,1,0:T(8,128)} %fusion.33), kind=kLoop, calls=%fused_computation.79 | loop fusion | flops 15040512 | bytes 37158912 | tf_op jit(solution)/shard_map/convert_element_type | solution.py:121
  144.6 22.6 %fusion.110 = f32[8,12,8,8,9,256]{5,3,2,1,0,4:T(8,128)} fusion(bf16[9,256,256,1,1,1]{2,1,5,4,3,0:T(8,128)(2,1)} %bitcast.400, bf16[8,12,1,8,256]{4,3,2,1,0:T(8,128)(2,1)} %copy.300, bf16[8,12,6,1,256]{4,3,2,1,0:T(2,128)(2,1)S(1)} %copy.295, bf16[8,12,6,6,256]{4,3,2,1,0:T(8,128)(2,1)S(1)} %get-tuple-element.164, bf16[8,12,6,1,256]{4,3,2,1,0:T(2,128)(2,1)S(1)} %copy.294, ...), kind=kOutput, calls=%fused_computation.208 | convolution fusion | flops 7263485952 | bytes 60948480 | tf_op jit(solution)/shard_map/pc,tcd->ptd/dot_general | solution.py:82
  167.2 18.1 %fusion.7 = (bf16[8,12,6,6,256]{4,3,2,1,0:T(8,128)(2,1)S(1)}, f32[8,12,6,6,1,256]{5,3,2,1,0,4:T(8,128)}) fusion(bf16[8]{0:T(256)(128)(2,1)S(1)} %copy-done.33, bf16[1,8,12,6,6,256]{5,1,4,3,2,0:T(8,128)(2,1)S(1)} %copy-done.1, f32[8,12,8,8,9,256]{5,3,2,1,0,4:T(8,128)} %fusion.110), kind=kLoop, calls=%fused_computation.20 | loop fusion | flops 26542080 | bytes 38928400 | tf_op jit(solution)/shard_map/convert_element_type | solution.py:187
  185.3 19.7 %fusion.36 = f32[8,12,6,6,9,256]{5,3,2,1,0,4:T(8,128)} fusion(bf16[9,256,256,1,1,1]{2,1,5,4,3,0:T(8,128)(2,1)S(1)} %bitcast.401, f32[8,12,6,6,1,256]{5,3,2,1,0,4:T(8,128)} %get-tuple-element.163, bf16[1,8,12,6,6,256]{5,1,4,3,2,0:T(8,128)(2,1)} %param.30, bf16[8]{0:T(256)(128)(2,1)} %copy-done.32), kind=kOutput, calls=%fused_computation.110 | convolution fusion | flops 4098097152 | bytes 38338576 | tf_op jit(solution)/shard_map/pd,tcd->ptc/dot_general | solution.py:97
  205.0 30.6 %slice_bitcast_fusion.17 = (f32[8,12,6,6,256]{4,3,2,1,0:T(8,128)}, f32[8,12,6,6,256]{4,3,2,1,0:T(8,128)}, f32[8,12,6,6,256]{4,3,2,1,0:T(8,128)}, f32[8,12,6,6,25...) fusion(f32[8,12,6,6,9,256]{5,3,2,1,0,4:T(8,128)} %fusion.36), kind=kLoop, calls=%fused_computation.57 | loop fusion | bytes 63700992 | tf_op jit(solution)/shard_map/squeeze | solution.py:103
  235.6 18.5 %pad_add_fusion.1 = f32[8,12,8,8,256]{4,3,2,1,0:T(8,128)} fusion(f32[8,12,6,6,256]{4,3,2,1,0:T(8,128)} %get-tuple-element.185, f32[8,12,6,6,256]{4,3,2,1,0:T(8,128)} %get-tuple-element.178, f32[8,12,6,6,256]{4,3,2,1,0:T(8,128)} %get-tuple-element.179, f32[8,12,6,6,256]{4,3,2,1,0:T(8,128)} %get-tuple-element.180, f32[8,12,6,6,256]{4,3,2,1,0:T(8,128)} %get-tuple-element.181, ...), kind=kLoop, calls=%fused_computation.7 | loop fusion | flops 12582912 | bytes 38141952 | tf_op jit(solution)/shard_map/add | solution.py:104
  254.1 4.9 fusion.169
  261.7 5.3 slice.563
  288.7 13.9 %bitcast_convert_fusion = bf16[9,256,256]{1,2,0:T(8,128)(2,1)} fusion(bf16[8,12,8,8,9,256]{5,3,2,1,0,4:T(8,128)(2,1)} %bitcast_dynamic-update-slice_fusion, bf16[8,12,1,8,256]{4,3,2,1,0:T(8,128)(2,1)S(1)} %copy-done.20, bf16[8,12,6,1,256]{4,3,2,1,0:T(2,128)(2,1)S(1)} %copy-done.18, bf16[8,12,6,6,256]{4,3,2,1,0:T(8,128)(2,1)S(1)} %copy-done.3, ...), kind=kOutput, calls=%fused_computation.108 | convolution fusion | flops 7264075776 | bytes 32636928 | tf_op jit(solution)/shard_map/pc,ptd->tcd/dot_general | solution.py:108
  307.7 3.2 slice_add_fusion.19
  310.9 13.4 %scatter-add.29 = f32[8,12,6,6,256]{4,3,2,1,0:T(8,128)} dynamic-update-slice(f32[8,12,6,6,256]{4,3,2,1,0:T(8,128)} %fusion.85, f32[8,12,6,1,256]{4,3,2,1,0:T(1,128)S(1)} %slice_add_fusion.19, s32[]{:T(128)} %constant.253.clone.1, s32[]{:T(128)} %constant.253.clone.1, s32[]{:T(128)} %constant.253.clone.1, s32[]{:T(128)} %constant.253.clone.1, s32[]{:T(128)} %constant.253.clone.1) | dynamic-update-slice | bytes 1179652 | tf_op jit(solution)/shard_map/scatter-add | solution.py:65
  326.8 3.4 slice_add_fusion.18
  330.2 12.9 %scatter-add.31 = f32[8,12,6,6,256]{4,3,2,1,0:T(8,128)} dynamic-update-slice(f32[8,12,6,6,256]{4,3,2,1,0:T(8,128)} %fusion.84, f32[8,12,6,1,256]{4,3,2,1,0:T(1,128)S(1)} %slice_add_fusion.18, s32[]{:T(128)} %constant.253.clone.1, s32[]{:T(128)} %constant.253.clone.1, s32[]{:T(128)} %constant.253.clone.1, s32[]{:T(128)} %constant.263.clone.1, s32[]{:T(128)} %constant.253.clone.1) | dynamic-update-slice | bytes 1179652 | tf_op jit(solution)/shard_map/scatter-add | solution.py:71
  343.1 5.5 %fusion.16 = bf16[8,12,6,6,256]{4,3,2,1,0:T(8,128)(2,1)S(1)} fusion(f32[8,12,6,6,256]{4,3,2,1,0:T(8,128)} %get-tuple-element.165, f32[8,12,6,6,256]{4,3,2,1,0:T(8,128)} %scatter-add.31), kind=kLoop, calls=%fused_computation.29 | loop fusion | flops 17694720 | bytes 8847360 | tf_op jit(solution)/shard_map/convert_element_type | solution.py:191
  370.2 16.7 %fusion.41 = f32[8,12,6,6,9,256]{5,1,4,3,2,0:T(8,128)} fusion(bf16[9,256,256,1,1,1]{2,1,0,5,4,3:T(8,128)(2,1)S(1)} %bitcast.403, bf16[8,12,6,6,256,1]{4,3,2,1,0,5:T(8,128)(2,1)S(1)} %bitcast.394), kind=kOutput, calls=%fused_computation.115 | convolution fusion | flops 4076863488 | bytes 34799616 | tf_op jit(solution)/shard_map/pd,tcd->ptc/dot_general | solution.py:97
  386.9 31.6 %slice_bitcast_fusion.8 = (f32[8,12,6,6,256]{4,1,3,2,0:T(8,128)}, f32[8,12,6,6,256]{4,1,3,2,0:T(8,128)}, f32[8,12,6,6,256]{4,1,3,2,0:T(8,128)}, f32[8,12,6,6,256...) fusion(f32[8,12,6,6,9,256]{5,1,4,3,2,0:T(8,128)} %fusion.41), kind=kLoop, calls=%fused_computation.48 | loop fusion | bytes 63700992 | tf_op jit(solution)/shard_map/squeeze | solution.py:103
  418.5 15.3 %bitcast_convert_fusion.1 = bf16[9,256,256]{1,2,0:T(8,128)(2,1)} fusion(bf16[8,12,8,8,9,256]{5,3,2,1,0,4:T(8,128)(2,1)} %bitcast_dynamic-update-slice_fusion.9, bf16[8,12,8,8,256,1]{4,1,3,0,2,5:T(8,128)(2,1)} %maximum_bitcast_fusion), kind=kOutput, calls=%fused_computation.109 | convolution fusion | flops 7248347136 | bytes 32636928 | tf_op jit(solution)/shard_map/pc,ptd->tcd/dot_general | solution.py:108
  433.9 5.4 %fusion.29 = bf16[1,8,12,6,6,256]{5,4,3,2,1,0:T(8,128)(2,1)S(1)} fusion(f32[1,8,12,6,6,256]{5,4,3,2,1,0:T(8,128)} %reshape.701, f32[8,12,6,6,1,256]{5,3,2,1,0,4:T(8,128)} %get-tuple-element.163), kind=kLoop, calls=%fused_computation.77 | loop fusion | flops 8847360 | bytes 8847360 | tf_op jit(solution)/shard_map/convert_element_type | solution.py:172
  439.3 3.1 copy.351
  442.4 15.0 %pad_add_fusion = f32[8,12,8,8,256]{4,1,3,2,0:T(8,128)S(1)} fusion(f32[8,12,6,6,256]{4,1,3,2,0:T(8,128)} %get-tuple-element.175, f32[8,12,6,6,256]{4,1,3,2,0:T(8,128)} %get-tuple-element.176, f32[8,12,6,6,256]{4,1,3,2,0:T(8,128)} %get-tuple-element.169, f32[8,12,6,6,256]{4,1,3,2,0:T(8,128)} %get-tuple-element.170, f32[8,12,6,6,256]{4,1,3,2,0:T(8,128)} %get-tuple-element.171, ...), kind=kLoop, calls=%fused_computation | loop fusion | flops 12582912 | bytes 38141952 | tf_op jit(solution)/shard_map/add | solution.py:104
  469.3 3.3 add_bitcast_fusion
  472.6 3.8 copy.352
  476.5 47.0 %all-reduce.43.cloned.1.call-done = (bf16[576,256]{1,0:T(8,128)(2,1)}, bf16[576,256]{1,0:T(8,128)(2,1)}) async-done(((bf16[576,256]{1,0:T(8,128)(2,1)}, bf16[576,256]{1,0:T(8,128)(2,1)}), (bf16[576,256]{1,0:T(8,128)(2,1)}, bf16[576,256]{1,0:T(8,128)(2,1)})) %all-reduce.43.cloned.1.call-update) | async-done | bytes 589840 | tf_op jit(solution)/shard_map/psum | solution.py:211
  (163 shorter events, 98.8 us)
Async XLA Ops:
  7.2 65.5 %reduce-scatter.10.cloned.1.call-start = ((), (), s32[]{:S(2)}) async-start(), calls=%async_computation.7 | async-start | bytes 163840 | tf_op jit(solution)/shard_map/reduce_scatter | solution.py:204
  7.9 19.4 %copy-start.32 = (bf16[8]{0:T(256)(128)(2,1)}, bf16[8]{0:T(256)(128)(2,1)S(1)}, u32[]{:S(2)}) copy-start(bf16[8]{0:T(256)(128)(2,1)S(1)} %compare_convert_fusion) | copy-start | bytes 52
  7.9 5.9 %copy-start.12 = (f32[576,256]{1,0:T(8,128)S(1)}, f32[576,256]{1,0:T(8,128)}, u32[]{:S(2)}) copy-start(f32[576,256]{1,0:T(8,128)} %param.33) | copy-start | bytes 1769476
  7.9 6.8 %copy-start.28 = (f32[64,256]{1,0:T(8,128)S(1)}, f32[64,256]{1,0:T(8,128)}, u32[]{:S(2)}) copy-start(f32[64,256]{1,0:T(8,128)} %param.35) | copy-start | bytes 196612
  7.9 15.0 %copy-start.6 = (bf16[1,8,12,6,6,256]{5,1,4,3,2,0:T(8,128)(2,1)S(1)}, bf16[1,8,12,6,6,256]{5,1,4,3,2,0:T(8,128)(2,1)}, u32[]{:S(2)}) copy-start(bf16[1,8,12,6,6,256]{5,1,4,3,2,0:T(8,128)(2,1)} %param.29) | copy-start | bytes 5308420
  13.8 83.5 %all-gather.3.cloned.1.call-start = ((), (), s32[]{:S(2)}) async-start(), calls=%async_computation.3 | async-start | bytes 1474560 | tf_op jit(solution)/shard_map/all_gather | solution.py:163
  14.6 129.2 %all-gather.5.cloned.1.call-start = ((), (), s32[]{:S(2)}) async-start(), calls=%async_computation.4 | async-start | bytes 1474560 | tf_op jit(solution)/shard_map/all_gather | solution.py:164
  15.9 11.3 %copy-start = (bf16[1,8,12,6,6,256]{5,1,4,3,2,0:T(8,128)(2,1)S(1)}, bf16[1,8,12,6,6,256]{5,1,4,3,2,0:T(8,128)(2,1)}, u32[]{:S(2)}) copy-start(bf16[1,8,12,6,6,256]{5,1,4,3,2,0:T(8,128)(2,1)} %param.30) | copy-start | bytes 5308420
  16.0 43.2 %collective-permute-start.1 = (bf16[64,256]{1,0:T(8,128)(2,1)}, bf16[64,256]{1,0:T(8,128)(2,1)}, u32[]{:S(2)}, u32[]{:S(2)}) collective-permute-start(bf16[64,256]{1,0:T(8,128)(2,1)} %get-tuple-element.167), channel_id=1, source_target_pairs={{0,3},{1,0},{2,1},{3,2},{4,7},{5,4},{6,5},{7,6},{8,11},{9,8},{10,9... | collective-permute-start | bytes 98312 | tf_op jit(solution)/shard_map/ppermute | solution.py:26
  21.0 36.6 %collective-permute-start = (bf16[64,256]{1,0:T(8,128)(2,1)}, bf16[64,256]{1,0:T(8,128)(2,1)}, u32[]{:S(2)}, u32[]{:S(2)}) collective-permute-start(bf16[64,256]{1,0:T(8,128)(2,1)} %get-tuple-element.167), channel_id=1, source_target_pairs={{0,1},{1,2},{2,3},{3,0},{4,5},{5,6},{6,7},{7,4},{8,9},{9,10},{10,1... | collective-permute-start | bytes 98312 | tf_op jit(solution)/shard_map/ppermute | solution.py:21
  22.8 446.4 %reduce-scatter.8.cloned.1.call-start = ((), (), s32[]{:S(2)}) async-start(), calls=%async_computation.6 | async-start | bytes 1474560 | tf_op jit(solution)/shard_map/reduce_scatter | solution.py:201
  29.4 5.4 copy-start.4
  38.5 19.8 %copy-start.27 = (bf16[256,256]{1,0:T(8,128)(2,1)S(1)}, bf16[256,256]{1,0:T(8,128)(2,1)}, u32[]{:S(2)}) copy-start(bf16[256,256]{1,0:T(8,128)(2,1)} %copy-done.26) | copy-start | bytes 393220
  38.5 25.6 %copy-start.7 = (bf16[3456,256]{1,0:T(8,128)(2,1)S(1)}, bf16[3456,256]{1,0:T(8,128)(2,1)}, u32[]{:S(2)}) copy-start(bf16[3456,256]{1,0:T(8,128)(2,1)} %reshape_squeeze.3) | copy-start | bytes 5308420
  57.6 6.6 %collective-permute-start.2 = (bf16[64,256]{1,0:T(8,128)(2,1)}, bf16[64,256]{1,0:T(8,128)(2,1)S(1)}, u32[]{:S(2)}, u32[]{:S(2)}) collective-permute-start(bf16[64,256]{1,0:T(8,128)(2,1)} %collective-permute-done), channel_id=1, source_target_pairs={{0,1},{1,2},{2,3},{3,0},{4,5},{5,6},{6,7},{7,4},{8,9},{9,10},{10,1... | collective-permute-start | bytes 98312 | tf_op jit(solution)/shard_map/ppermute | solution.py:21
  67.8 28.8 %copy-start.29 = (f32[64,256]{1,0:T(8,128)S(1)}, f32[64,256]{1,0:T(8,128)}, u32[]{:S(2)}) copy-start(f32[64,256]{1,0:T(8,128)} %param.35) | copy-start | bytes 196612
  67.8 28.8 %copy-start.30 = (f32[64,256]{1,0:T(8,128)S(1)}, f32[64,256]{1,0:T(8,128)}, u32[]{:S(2)}) copy-start(f32[64,256]{1,0:T(8,128)} %param.40) | copy-start | bytes 196612
  67.8 28.8 %copy-start.31 = (f32[64,256]{1,0:T(8,128)S(1)}, f32[64,256]{1,0:T(8,128)}, u32[]{:S(2)}) copy-start(f32[64,256]{1,0:T(8,128)} %param.41) | copy-start | bytes 196612
  138.3 5.5 %copy-start.2 = (bf16[8,12,6,6,256]{4,3,2,1,0:T(8,128)(2,1)}, bf16[8,12,6,6,256]{4,3,2,1,0:T(8,128)(2,1)S(1)}, u32[]{:S(2)}) copy-start(bf16[8,12,6,6,256]{4,3,2,1,0:T(8,128)(2,1)S(1)} %get-tuple-element.164) | copy-start | bytes 5308420
  144.6 22.7 %copy-start.1 = (bf16[1,8,12,6,6,256]{5,1,4,3,2,0:T(8,128)(2,1)S(1)}, bf16[1,8,12,6,6,256]{5,1,4,3,2,0:T(8,128)(2,1)}, u32[]{:S(2)}) copy-start(bf16[1,8,12,6,6,256]{5,1,4,3,2,0:T(8,128)(2,1)} %param.30) | copy-start | bytes 5308420
  144.6 22.7 %copy-start.33 = (bf16[8]{0:T(256)(128)(2,1)S(1)}, bf16[8]{0:T(256)(128)(2,1)}, u32[]{:S(2)}) copy-start(bf16[8]{0:T(256)(128)(2,1)} %copy-done.32) | copy-start | bytes 52
  167.2 18.1 %copy-start.8 = (bf16[2304,256]{1,0:T(8,128)(2,1)S(1)}, bf16[2304,256]{1,0:T(8,128)(2,1)}, u32[]{:S(2)}) copy-start(bf16[2304,256]{1,0:T(8,128)(2,1)} %all-gather.5.cloned.1.call-done) | copy-start | bytes 3538948
  302.7 166.6 %reduce-scatter.6.cloned.1.call-start = ((), (), s32[]{:S(2)}) async-start(), calls=%async_computation.5 | async-start | bytes 1474560 | tf_op jit(solution)/shard_map/reduce_scatter | solution.py:198
  433.8 89.6 %all-reduce.43.cloned.1.call-start = ((), (), s32[]{:S(2)}) async-start(), calls=%async_computation.8 | async-start | bytes 1179648 | tf_op jit(solution)/shard_map/psum | solution.py:211
  460.1 9.1 %copy-start.5 = (bf16[8,12,6,6,256]{4,3,2,1,0:T(8,128)(2,1)S(1)}, bf16[8,12,6,6,256]{4,3,2,1,0:T(8,128)(2,1)}, u32[]{:S(2)}) copy-start(bf16[8,12,6,6,256]{4,3,2,1,0:T(8,128)(2,1)} %fusion.35) | copy-start | bytes 5308420
  460.2 9.1 %copy-start.25 = (bf16[256,256]{1,0:T(8,128)(2,1)S(1)}, bf16[256,256]{1,0:T(8,128)(2,1)}, u32[]{:S(2)}) copy-start(bf16[256,256]{1,0:T(8,128)(2,1)} %all_gather.13) | copy-start | bytes 393220
  472.6 50.9 %copy-start.13 = (f32[576,256]{1,0:T(8,128)S(1)}, f32[576,256]{1,0:T(8,128)}, u32[]{:S(2)}) copy-start(f32[576,256]{1,0:T(8,128)} %param.33) | copy-start | bytes 1769476
  472.6 50.9 %copy-start.21 = (f32[576,256]{1,0:T(8,128)S(1)}, f32[576,256]{1,0:T(8,128)}, u32[]{:S(2)}) copy-start(f32[576,256]{1,0:T(8,128)} %param.36) | copy-start | bytes 1769476
  472.6 50.9 %copy-start.22 = (f32[576,256]{1,0:T(8,128)S(1)}, f32[576,256]{1,0:T(8,128)}, u32[]{:S(2)}) copy-start(f32[576,256]{1,0:T(8,128)} %param.37) | copy-start | bytes 1769476
  472.6 53.3 %copy-start.14 = (f32[576,256]{1,0:T(8,128)S(1)}, f32[576,256]{1,0:T(8,128)}, u32[]{:S(2)}) copy-start(f32[576,256]{1,0:T(8,128)} %param.34) | copy-start | bytes 1769476
  472.6 53.3 %copy-start.23 = (f32[576,256]{1,0:T(8,128)S(1)}, f32[576,256]{1,0:T(8,128)}, u32[]{:S(2)}) copy-start(f32[576,256]{1,0:T(8,128)} %param.38) | copy-start | bytes 1769476
  472.6 53.3 %copy-start.24 = (f32[576,256]{1,0:T(8,128)S(1)}, f32[576,256]{1,0:T(8,128)}, u32[]{:S(2)}) copy-start(f32[576,256]{1,0:T(8,128)} %param.39) | copy-start | bytes 1769476
  (12 other events, 39.2 us)
Sparse Core Ops, SparseCore 0:
  13.9 21.8 reduce-scatter.9
  38.0 30.5 all-gather.2
  70.8 30.1 all-gather.4
  302.8 27.9 reduce-scatter.7
  434.0 28.1 reduce-scatter.5
  469.4 54.0 all-reduce.42
